TPU v7x, 256 devices: a whole 4x4x8 slice. The times are simulated.
256 devices in a mesh: seq: 32 (over x, z), tensor: 8 (over y, core).
Axes of the slice: x: 4, y: 4, z: 8, core: 2. Of those that a mesh axis runs over, the one named last changes fastest.
Arguments:
- hidden_in: bfloat16 [8192, 4096], P(('seq', 'tensor')), may hold values from -30 to 30
- prev_amax: float32 [], replicated, may hold values from 5 to 9
- w_x: bfloat16 [4096, 8192], P('seq', 'tensor'), may hold values from -0.09375 to 0.09375
- w_bc: bfloat16 [4096, 8, 2, 128], P('seq', 'tensor'), may hold values from -0.046875 to 0.046875
- w_dt: bfloat16 [4096, 128], P('seq', 'tensor'), may hold values from -0.09375 to 0.09375
- conv_x: float32 [4, 8192], P(None, 'tensor'), may hold values from -4 to 4
- conv_bc: float32 [4, 8, 2, 128], P(None, 'tensor'), may hold values from -4 to 4
- conv_state_x: bfloat16 [3, 8192], P(None, 'tensor'), may hold values from -6 to 6
- conv_state_bc: bfloat16 [3, 8, 2, 128], P(None, 'tensor'), may hold values from -3 to 3
- dt_bias: float32 [128], P('tensor'), may hold values from -2 to 1
- decay_rate: float32 [128], P('tensor'), may hold values from 1.2207031e-05 to 0.12
- skip: float32 [128], P('tensor'), may hold values from 0.5 to 4
- init_state: float32 [128, 64, 128], P('tensor'), may hold values from -48 to 48
- norm_gain: float32 [8192], P('tensor'), may hold values from 0.1 to 1.9
- w_out: bfloat16 [8192, 4096], P('tensor', 'seq'), may hold values from -0.0625 to 0.0625
Outputs:
- layer_out: bfloat16 [8192, 4096], P(('seq', 'tensor'))
- abs_max: float32 [], replicated
All inputs are finite; a program needn't handle non-finite values.
Results may differ from a plain program's by a relative error of at most 0.019.
Values may be sent and summed in bfloat16 or wider, within the bound.
A program may use at most 64 MiB of HBM per device.

v0:
```python
import jax
import jax.numpy as jnp
from jax import lax
from jax.sharding import Mesh
from jax.sharding import PartitionSpec as P

HEADS = 128
HEAD_DIM = 64
STATE = 128
GROUPS = 8
KERNEL = 4
SPAN = 128
SEQ = ("seq_0", "seq_1")
SEQ_TENSOR = ("seq_0", "seq_1", "tensor")
epsilon = 1e-05
quant_range = 448.0


def in_order(parts, dim):
    dims = list(parts.shape[1:])
    dims[dim] *= parts.shape[0]
    return jnp.moveaxis(parts, 0, dim).reshape(dims)


def sent_to_all(shard, axis):
    count = lax.axis_size(axis)
    return lax.all_to_all(
        jnp.broadcast_to(shard[None], (count, *shard.shape)), axis, 0, 0, tiled=True
    )


def gather_directly(shard, axis, dim):
    return in_order(sent_to_all(shard, axis), dim)


def over_copies(shard, axis):
    everything = sent_to_all(shard, axis)
    return jnp.max(everything, axis=0)


def sent_together(arrays, axis, dim, along):
    ends, at = ([], 0)
    for a in arrays[:-1]:
        at += a.shape[along]
        ends.append(at)
    both = jnp.concatenate(arrays, axis=along)
    return tuple(jnp.split(lax.all_gather(both, axis, axis=dim, tiled=True), ends, axis=along))


def from_behind(value, axis, steps):
    count = lax.axis_size(axis)
    first, last = (max(0, -steps), min(count, count - steps))
    return lax.ppermute(value, axis, [(source, source + steps) for source in range(first, last)])


def neutral_like(shard, identity):
    return jax.tree.map(
        lambda a, e: jnp.broadcast_to(jnp.asarray(e, a.dtype), a.shape), shard, identity
    )


def prefix_by_axis(shard, axes, combine, identity):
    before = start = neutral_like(shard, identity)
    total = shard
    for axis in reversed(axes):
        count, here = (lax.axis_size(axis), lax.axis_index(axis))
        pieces = jax.tree.map(
            lambda part, kind: lax.all_gather(part.astype(kind), axis),
            total,
            (jnp.bfloat16, jnp.bfloat16),
        )
        inside, total = (start, start)
        for k in range(count):
            passed = k < here
            total = combine(
                total, jax.tree.map(lambda part, own: part[k].astype(own.dtype), pieces, shard)
            )
            inside = jax.tree.map(lambda new, old: jnp.where(passed, new, old), total, inside)
        before = combine(inside, before)
    return before


def taken_together(shard, axis):
    return sent_to_all(shard, axis).sum(axis=0)


def cut_along(shard, dim, count):
    before, after = (shard.shape[:dim], shard.shape[dim + 1 :])
    return jnp.moveaxis(shard.reshape(*before, count, -1, *after), dim, 0)


def sent_and_summed(shard, axis, dim):
    parts = cut_along(shard, dim, lax.axis_size(axis))
    arrived = lax.all_to_all(parts, axis, split_axis=0, concat_axis=0, tiled=True)
    return arrived.astype(jnp.float32).sum(axis=0)


def depthwise(before, projected, conv_taps, length):
    extended = jnp.concatenate([before, projected], axis=0)
    summed = conv_taps[0] * extended[0:length]
    for offset in range(1, KERNEL):
        summed = summed + conv_taps[offset] * extended[offset : offset + length]
    return jax.nn.silu(summed).astype(jnp.bfloat16)


def combine(earlier, later):
    return (earlier[0] * later[0], later[0][:, None, None] * earlier[1] + later[1])


def local(
    hidden_in,
    prev_amax,
    w_x,
    w_bc,
    w_dt,
    conv_x,
    conv_bc,
    conv_state_x,
    conv_state_bc,
    dt_bias,
    decay_rate,
    skip,
    init_state,
    norm_gain,
    w_out,
):
    margin = KERNEL - 1
    gathered = gather_directly(hidden_in, "tensor", 0)
    abs_max = over_copies(jnp.max(jnp.abs(gathered.astype(jnp.float32))), SEQ)
    in_scale = prev_amax / quant_range
    leading = lax.axis_index(SEQ) == 0
    row_count = gathered.shape[0]
    bc_width = w_bc.shape[1] * w_bc.shape[2] * w_bc.shape[3]
    bc_rows = jnp.reshape(w_bc, (w_bc.shape[0], bc_width))
    scaled = gathered.astype(jnp.float32) * (quant_range / prev_amax)
    quant = jnp.clip(scaled, -quant_range, quant_range).astype(jnp.bfloat16)
    pieces = sent_together((w_x, bc_rows, w_dt), SEQ, 0, 1)
    x_proj, bc_proj, dt_proj = tuple(
        (
            jnp.dot(quant, weight_piece, preferred_element_type=jnp.float32)
            for weight_piece in pieces
        )
    )
    x_whole = (x_proj * in_scale).astype(jnp.bfloat16)
    bc_whole = (bc_proj * in_scale).astype(jnp.bfloat16)
    dt_raw = dt_proj * in_scale
    state_bc = jnp.reshape(conv_state_bc, (margin, bc_width))
    received = from_behind((x_whole[row_count - margin :], bc_whole[row_count - margin :]), SEQ, 1)
    x_edge = jnp.where(leading, conv_state_x, received[0])
    bc_edge = jnp.where(leading, state_bc, received[1])
    x_act = depthwise(x_edge, x_whole, conv_x, row_count)
    bc_act = depthwise(bc_edge, bc_whole, jnp.reshape(conv_bc, (KERNEL, bc_width)), row_count)
    step_size = jax.nn.softplus(dt_raw + dt_bias)
    heads_here = step_size.shape[1]
    groups_here = w_bc.shape[1]
    per_group = HEADS // GROUPS
    blocks = row_count // SPAN
    x_blocks = x_act.reshape(blocks, SPAN, heads_here, HEAD_DIM)
    bc_blocks = bc_act.reshape(blocks, SPAN, groups_here, 2, STATE)
    in_map = bc_blocks[:, :, :, 0]
    out_map = bc_blocks[:, :, :, 1]
    step_blocks = step_size.reshape(blocks, SPAN, heads_here)
    cum_blocks = jnp.cumsum(-step_blocks * decay_rate, axis=1)
    index_row = jnp.arange(SPAN, dtype=jnp.int32)
    lower_mask = index_row[:, None] >= index_row[None, :]
    intersection = jnp.einsum(
        "ctgn,cugn->cgtu", out_map, in_map, preferred_element_type=jnp.float32
    )
    intersection = jnp.repeat(intersection, per_group, axis=1)
    cum_heads = jnp.transpose(cum_blocks, (0, 2, 1))
    log_gap = cum_heads[:, :, :, None] - cum_heads[:, :, None, :]
    decay = jnp.exp(jnp.where(lower_mask[None, None], log_gap, -1e30))
    step_heads = jnp.transpose(step_blocks, (0, 2, 1))
    weights = (intersection * decay * step_heads[:, :, None, :]).astype(jnp.bfloat16)
    local_part = jnp.einsum(
        "chtu,cuhp->cthp", weights, x_blocks, preferred_element_type=jnp.float32
    )
    last_cum = cum_blocks[:, SPAN - 1, :]
    x_weighted = (
        x_blocks.astype(jnp.float32)
        * (step_blocks * jnp.exp(last_cum[:, None, :] - cum_blocks))[:, :, :, None]
    ).astype(jnp.bfloat16)
    in_heads = jnp.repeat(in_map, per_group, axis=2)
    added = jnp.einsum("cuhp,cuhn->chpn", x_weighted, in_heads, preferred_element_type=jnp.float32)

    def carry_on(carried, element):
        block_decay, block_added = element
        return (block_decay[:, None, None] * carried + block_added, carried)

    empty_state = jnp.zeros((heads_here, HEAD_DIM, STATE), jnp.float32)
    device_state, entering = lax.scan(carry_on, empty_state, (jnp.exp(last_cum), added))
    device_decay = jnp.exp(jnp.sum(last_cum, axis=0))
    seeded = device_state + jnp.where(leading, device_decay[:, None, None] * init_state, 0.0)
    identity = (jnp.ones_like(device_decay), jnp.zeros_like(device_state))
    scanned = prefix_by_axis((device_decay, seeded), SEQ, combine, identity)
    incoming = jnp.where(leading, init_state, scanned[1])
    prefix = jnp.exp(jnp.cumsum(last_cum, axis=0) - last_cum)
    states_in = entering + prefix[:, :, None, None] * incoming[None]
    out_heads = jnp.repeat(out_map, per_group, axis=2).astype(jnp.float32)
    carried_part = (
        jnp.einsum("cthn,chpn->cthp", out_heads, states_in, precision=lax.Precision.HIGHEST)
        * jnp.exp(cum_blocks)[:, :, :, None]
    )
    ssm_out = local_part + carried_part + skip[None, None, :, None] * x_blocks.astype(jnp.float32)
    ssm_out = ssm_out.reshape(row_count, heads_here * HEAD_DIM)
    squares = taken_together(jnp.sum(ssm_out * ssm_out, axis=1), "tensor")
    mean_sq = squares / (HEADS * HEAD_DIM)
    normed = (ssm_out * lax.rsqrt(mean_sq + epsilon)[:, None] * norm_gain).astype(jnp.bfloat16)
    partial_out = jnp.dot(
        normed, lax.all_gather(w_out, SEQ, axis=1, tiled=True), preferred_element_type=jnp.float32
    )
    layer_out = sent_and_summed(partial_out.astype(jnp.bfloat16), "tensor", 0).astype(jnp.bfloat16)
    return (layer_out, abs_max)


def solution(mesh):
    finer = Mesh(mesh.devices.reshape(4, 8, mesh.shape["tensor"]), ("seq_0", "seq_1", "tensor"))
    return jax.shard_map(
        local,
        mesh=finer,
        in_specs=(
            P(SEQ_TENSOR, None),
            P(),
            P(SEQ, "tensor"),
            P(SEQ, "tensor", None, None),
            P(SEQ, "tensor"),
            P(None, "tensor"),
            P(None, "tensor", None, None),
            P(None, "tensor"),
            P(None, "tensor", None, None),
            P("tensor"),
            P("tensor"),
            P("tensor"),
            P("tensor", None, None),
            P("tensor"),
            P("tensor", SEQ),
        ),
        out_specs=(P(SEQ_TENSOR, None), P()),
        check_vma=False,
    )
```

profile of v0, /device:TPU:1, one launch (start us, length us, event | category | flops | bytes accessed | tf_op | source)
XLA Modules:
  0.0 373.7 jit_solution(1133156709951974368)
XLA Ops:
  7.2 0.9 copy.100
  8.1 0.8 copy.69
  8.9 1.7 pad_maximum_fusion.1
  10.6 2.6 broadcast_in_dim.26
  13.2 6.8 %all-to-all-start = ((bf16[8,32,4096]{2,1,0:T(8,128)(2,1)}), bf16[8,32,4096]{2,1,0:T(8,128)(2,1)S(1)}, u32[]{:S(2)}, u32[]{:S(2)}) async-start(bf16[8,32,4096]{2,1,0:T(8,128)(2,1)} %broadcast_in_dim.26), calls=%async_computation | async-start | bytes 4194304 | tf_op jit(solution)/shard_map/all_to_all | solution.py:27
  20.8 25.5 %all-to-all-done = bf16[8,32,4096]{2,1,0:T(8,128)(2,1)S(1)} async-done(((bf16[8,32,4096]{2,1,0:T(8,128)(2,1)}), bf16[8,32,4096]{2,1,0:T(8,128)(2,1)S(1)}, u32[]{:S(2)}, u32[]{:S(2)}) %all-to-all-start) | async-done | bytes 2097184 | tf_op jit(solution)/shard_map/all_to_all | solution.py:27
  46.3 2.6 fusion.5
  48.9 78.4 %all-gather.8.cloned.1.call-done = bf16[4096,1296]{1,0:T(8,128)(2,1)} async-done(((bf16[128,1296]{1,0:T(8,128)(2,1)}), bf16[4096,1296]{1,0:T(8,128)(2,1)}) %all-gather.8.cloned.1.call-update) | async-done | bytes 10616848 | tf_op jit(solution)/shard_map/all_gather | solution.py:47
  127.3 2.7 compare_select_fusion
  130.4 0.7 fusion.95
  131.1 2.3 fusion.20
  133.4 0.6 copy-done.5
  134.1 1.5 collective-permute-start.1
  135.6 5.7 %fusion.14 = bf16[256,1024]{1,0:T(8,128)(2,1)S(1)} fusion(bf16[256,4096]{1,0:T(8,128)(2,1)S(1)} %bitcast.201, bf16[4096,1296]{1,0:T(8,128)(2,1)} %all-gather.8.cloned.1.call-done, f32[]{:T(128)S(6)} %div.21), kind=kOutput, calls=%fused_computation.23 | convolution fusion | flops 2148007936 | bytes 11010052 | tf_op jit(solution)/shard_map/dot_general | solution.py:140
  141.3 3.2 collective-permute-start
  144.5 0.6 subtract_exponential_fusion
  145.1 1.0 copy.80
  146.1 1.3 multiply_convert_fusion.3
  147.5 0.8 fusion.96
  148.4 0.7 multiply_convert_fusion.2
  149.1 0.7 reshape.405
  149.8 0.9 copy.77
  151.0 2.0 while.13
  151.1 0.8 bitcast_dynamic-update-slice_fusion.2
  152.1 0.8 bitcast_dynamic-update-slice_fusion.2
  153.0 0.8 add_convert_fusion
  155.4 13.2 %all-reduce = bf16[128]{0:T(256)(128)(2,1)S(1)} all-reduce(bf16[128]{0:T(256)(128)(2,1)S(1)} %dynamic-update-slice), channel_id=2, replica_groups=mesh['seq_0'=4,'seq_1'=8,'tensor'=8] {'seq_1'}, use_global_device_ids=true, to_apply=%add | all-reduce | flops 128 | bytes 512
  168.6 0.7 broadcast_select_fusion.8
  169.3 20.5 %all-gather.14.cloned.1.call-done = bf16[128,64,128]{2,1,0:T(8,128)(2,1)} async-done(((bf16[16,64,128]{2,1,0:T(8,128)(2,1)}), bf16[128,64,128]{2,1,0:T(8,128)(2,1)}) %all-gather.14.cloned.1.call-update) | async-done | bytes 2097168 | tf_op jit(solution)/shard_map/all_gather | solution.py:68
  189.8 2.8 fusion.80
  193.3 8.1 %all-gather.2 = bf16[4,1,16]{2,1,0:T(2,128)(2,1)S(1)} all-gather(bf16[1,1,16]{2,1,0:T(2,128)(2,1)S(1)} %fusion.91), channel_id=1, replica_groups=mesh['seq_0'=4,'seq_1'=8,'tensor'=8] {'seq_0'}, dimensions={0}, use_global_device_ids=true | all-gather | bytes 160 | tf_op jit(solution)/shard_map/all_gather | solution.py:68
  201.6 1.1 copy.102
  202.8 1.9 convolution_bitcast_fusion.1
  204.8 15.7 %all-gather.10.cloned.1.call-done = bf16[4,16,64,128]{3,2,1,0:T(8,128)(2,1)} async-done(((bf16[1,16,64,128]{3,2,1,0:T(8,128)(2,1)}), bf16[4,16,64,128]{3,2,1,0:T(8,128)(2,1)}) %all-gather.10.cloned.1.call-update) | async-done | bytes 1048592 | tf_op jit(solution)/shard_map/all_gather | solution.py:68
  220.5 3.1 fusion.46
  223.7 2.2 multiply_reduce_fusion
  225.9 0.6 broadcast_in_dim.33
  226.5 7.1 %all-to-all-start.1 = ((f32[8,1,256]{2,1,0:T(1,128)}), f32[8,1,256]{2,1,0:T(1,128)S(1)}, u32[]{:S(2)}, u32[]{:S(2)}) async-start(f32[8,1,256]{2,1,0:T(1,128)} %broadcast_in_dim.33), calls=%async_computation.1 | async-start | bytes 16384 | tf_op jit(solution)/shard_map/all_to_all | solution.py:27
  233.5 0.8 copy.82
  234.4 3.8 %all-to-all-done.1 = f32[8,1,256]{2,1,0:T(1,128)S(1)} async-done(((f32[8,1,256]{2,1,0:T(1,128)}), f32[8,1,256]{2,1,0:T(1,128)S(1)}, u32[]{:S(2)}, u32[]{:S(2)}) %all-to-all-start.1) | async-done | bytes 8224 | tf_op jit(solution)/shard_map/all_to_all | solution.py:27
  238.2 1.3 broadcast_in_dim.35
  239.4 8.6 %all-to-all-start.3 = ((f32[32,1,1]{2,1,0:T(1,128)}), f32[32,1,1]{2,1,0:T(1,128)S(1)}, u32[]{:S(2)}, u32[]{:S(2)}) async-start(f32[32,1,1]{2,1,0:T(1,128)} %broadcast_in_dim.35), calls=%async_computation.3 | async-start | bytes 32768 | tf_op jit(solution)/shard_map/all_to_all | solution.py:27
  248.1 76.4 %all-gather.12.cloned.1.call-done = bf16[1024,4096]{1,0:T(8,128)(2,1)} async-done(((bf16[1024,128]{1,0:T(8,128)(2,1)}), bf16[1024,4096]{1,0:T(8,128)(2,1)}) %all-gather.12.cloned.1.call-update) | async-done | bytes 8388624 | tf_op jit(solution)/shard_map/all_gather | solution.py:210
  324.5 7.2 %convolution_convert_fusion = bf16[256,4096]{1,0:T(8,128)(2,1)} fusion(bf16[1024,4096]{1,0:T(8,128)(2,1)} %all-gather.12.cloned.1.call-done, f32[128,8,2,128]{3,2,1,0:T(2,128)S(1)} %bitcast.202, f32[1024]{0:T(1024)S(1)} %copy-done.6, f32[256]{0:T(256)S(1)} %add_rsqrt_fusion), kind=kOutput, calls=%fused_computation.8 | convolution fusion | flops 2149318656 | bytes 11539456 | tf_op jit(solution)/shard_map/dot_general | solution.py:209
  331.8 8.1 %all-to-all-start.2 = ((bf16[8,32,4096]{2,1,0:T(8,128)(2,1)}), bf16[8,32,4096]{2,1,0:T(8,128)(2,1)S(1)}, u32[]{:S(2)}, u32[]{:S(2)}) async-start(bf16[8,32,4096]{2,1,0:T(8,128)(2,1)} %bitcast.37), calls=%async_computation.2 | async-start | bytes 4194304 | tf_op jit(solution)/shard_map/all_to_all | solution.py:94
  339.9 0.6 reduce_max.19
  340.6 25.6 %all-to-all-done.2 = bf16[8,32,4096]{2,1,0:T(8,128)(2,1)S(1)} async-done(((bf16[8,32,4096]{2,1,0:T(8,128)(2,1)}), bf16[8,32,4096]{2,1,0:T(8,128)(2,1)S(1)}, u32[]{:S(2)}, u32[]{:S(2)}) %all-to-all-start.2) | async-done | bytes 2097184 | tf_op jit(solution)/shard_map/all_to_all | solution.py:94
  366.1 1.1 reduce_sum.42
  (84 shorter events, 3.3 us)
Async XLA Ops:
  7.2 120.2 %all-gather.8.cloned.1.call-start = ((), (), s32[]{:S(2)}) async-start(), calls=%async_computation.4 | async-start | bytes 11894784 | tf_op jit(solution)/shard_map/all_gather | solution.py:47
  13.2 7.5 %copy-start.11 = (f32[4,1,2,128]{3,2,1,0:T(2,128)S(1)}, f32[4,1,2,128]{3,2,1,0:T(2,128)}, u32[]{:S(2)}) copy-start(f32[4,1,2,128]{3,2,1,0:T(2,128)} %param.23) | copy-start | bytes 12292
  13.2 7.6 %copy-start.7 = (f32[4,1024]{1,0:T(4,128)S(1)}, f32[4,1024]{1,0:T(4,128)}, u32[]{:S(2)}) copy-start(f32[4,1024]{1,0:T(4,128)} %param.22) | copy-start | bytes 49156
  13.2 33.1 %all-to-all-start = ((bf16[8,32,4096]{2,1,0:T(8,128)(2,1)}), bf16[8,32,4096]{2,1,0:T(8,128)(2,1)S(1)}, u32[]{:S(2)}, u32[]{:S(2)}) async-start(bf16[8,32,4096]{2,1,0:T(8,128)(2,1)} %broadcast_in_dim.26), calls=%async_computation | async-start | bytes 4194304 | tf_op jit(solution)/shard_map/all_to_all | solution.py:27
  20.1 169.8 %all-gather.14.cloned.1.call-start = ((), (), s32[]{:S(2)}) async-start(), calls=%async_computation.7 | async-start | bytes 2359296 | tf_op jit(solution)/shard_map/all_gather | solution.py:68
  20.8 106.5 %copy-start.15 = (f32[16]{0:T(128)S(1)}, f32[16]{0:T(128)}, u32[]{:S(2)}) copy-start(f32[16]{0:T(128)} %param.26) | copy-start | bytes 196
  48.9 81.2 %copy-start.16 = (f32[16]{0:T(128)S(1)}, f32[16]{0:T(128)}, u32[]{:S(2)}) copy-start(f32[16]{0:T(128)} %param.27) | copy-start | bytes 196
  127.3 3.8 %copy-start = (bf16[8,32,4096]{2,1,0:T(8,128)(2,1)S(1)}, bf16[8,32,4096]{2,1,0:T(8,128)(2,1)}, u32[]{:S(2)}) copy-start(bf16[8,32,4096]{2,1,0:T(8,128)(2,1)} %get-tuple-element.61) | copy-start | bytes 6291460
  133.4 0.7 copy-start.5
  134.1 12.1 %copy-start.14 = (bf16[3,1,2,128]{3,2,1,0:T(2,128)(2,1)S(1)}, bf16[3,1,2,128]{3,2,1,0:T(2,128)(2,1)}, u32[]{:S(2)}) copy-start(bf16[3,1,2,128]{3,2,1,0:T(2,128)(2,1)} %param.25) | copy-start | bytes 4612
  134.1 14.3 %copy-start.8 = (bf16[3,1024]{1,0:T(4,128)(2,1)S(1)}, bf16[3,1024]{1,0:T(4,128)(2,1)}, u32[]{:S(2)}) copy-start(bf16[3,1024]{1,0:T(4,128)(2,1)} %param.24) | copy-start | bytes 18436
  134.1 12.0 %collective-permute-start.1 = (bf16[3,256]{1,0:T(4,128)(2,1)S(1)}, bf16[3,256]{1,0:T(4,128)(2,1)S(1)}, u32[]{:S(2)}, u32[]{:S(2)}) collective-permute-start(bf16[3,256]{1,0:T(4,128)(2,1)S(1)} %slice.201), channel_id=1, source_target_pairs={{0,8},{8,16},{16,24},{24,32},{32,40},{40,48},{48,56},{56,64},{64,7... | collective-permute-start | bytes 4616 | tf_op jit(solution)/shard_map/ppermute | solution.py:53
  141.3 7.0 %collective-permute-start = (bf16[3,1024]{1,0:T(4,128)(2,1)S(1)}, bf16[3,1024]{1,0:T(4,128)(2,1)S(1)}, u32[]{:S(2)}, u32[]{:S(2)}) collective-permute-start(bf16[3,1024]{1,0:T(4,128)(2,1)S(1)} %slice.196), channel_id=1, source_target_pairs={{0,8},{8,16},{16,24},{24,32},{32,40},{40,48},{48,56},{56,64},{64,7... | collective-permute-start | bytes 18440 | tf_op jit(solution)/shard_map/ppermute | solution.py:53
  151.0 2.0 copy-start.2
  151.0 3.0 copy-start.18
  153.9 66.6 %all-gather.10.cloned.1.call-start = ((), (), s32[]{:S(2)}) async-start(), calls=%async_computation.5 | async-start | bytes 1310720 | tf_op jit(solution)/shard_map/all_gather | solution.py:68
  169.2 32.2 %copy-start.9 = (f32[16]{0:T(128)}, f32[16]{0:T(128)S(1)}, u32[]{:S(2)}) copy-start(f32[16]{0:T(128)S(1)} %get-tuple-element.82) | copy-start | bytes 196
  192.6 131.9 %all-gather.12.cloned.1.call-start = ((), (), s32[]{:S(2)}) async-start(), calls=%async_computation.6 | async-start | bytes 8650752 | tf_op jit(solution)/shard_map/all_gather | solution.py:210
  201.6 18.9 %copy-start.1 = (bf16[128,64,128]{2,1,0:T(8,128)(2,1)S(1)}, bf16[128,64,128]{2,1,0:T(8,128)(2,1)}, u32[]{:S(2)}) copy-start(bf16[128,64,128]{2,1,0:T(8,128)(2,1)} %all-gather.14.cloned.1.call-done) | copy-start | bytes 6291460
  201.6 18.9 %copy-start.10 = (f32[16]{0:T(128)S(1)}, f32[16]{0:T(128)}, u32[]{:S(2)}) copy-start(f32[16]{0:T(128)} %copy-done.9) | copy-start | bytes 196
  201.6 18.9 %copy-start.13 = (f32[16]{0:T(128)S(1)}, f32[16]{0:T(128)}, u32[]{:S(2)}) copy-start(f32[16]{0:T(128)} %get-tuple-element.81) | copy-start | bytes 196
  220.5 3.2 copy-start.3
  220.5 3.2 copy-start.4
  220.5 3.2 copy-start.12
  220.5 3.2 copy-start.17
  225.9 98.6 %copy-start.6 = (f32[1024]{0:T(1024)S(1)}, f32[1024]{0:T(1024)}, u32[]{:S(2)}) copy-start(f32[1024]{0:T(1024)} %param.30) | copy-start | bytes 12292
  226.5 11.7 %all-to-all-start.1 = ((f32[8,1,256]{2,1,0:T(1,128)}), f32[8,1,256]{2,1,0:T(1,128)S(1)}, u32[]{:S(2)}, u32[]{:S(2)}) async-start(f32[8,1,256]{2,1,0:T(1,128)} %broadcast_in_dim.33), calls=%async_computation.1 | async-start | bytes 16384 | tf_op jit(solution)/shard_map/all_to_all | solution.py:27
  239.4 92.3 %all-to-all-start.3 = ((f32[32,1,1]{2,1,0:T(1,128)}), f32[32,1,1]{2,1,0:T(1,128)S(1)}, u32[]{:S(2)}, u32[]{:S(2)}) async-start(f32[32,1,1]{2,1,0:T(1,128)} %broadcast_in_dim.35), calls=%async_computation.3 | async-start | bytes 32768 | tf_op jit(solution)/shard_map/all_to_all | solution.py:27
  331.8 34.4 %all-to-all-start.2 = ((bf16[8,32,4096]{2,1,0:T(8,128)(2,1)}), bf16[8,32,4096]{2,1,0:T(8,128)(2,1)S(1)}, u32[]{:S(2)}, u32[]{:S(2)}) async-start(bf16[8,32,4096]{2,1,0:T(8,128)(2,1)} %bitcast.37), calls=%async_computation.2 | async-start | bytes 4194304 | tf_op jit(solution)/shard_map/all_to_all | solution.py:94
Sparse Core Ops, SparseCore 0:
  10.7 116.5 all-gather.7
  154.0 35.7 all-gather.13
  192.8 27.6 all-gather.9
  222.8 101.6 all-gather.11
where the time goes:
time: 375 us; the launch traced here: 374 us
  waiting for transfers between devices  247 us (66%)
  starting transfers between devices  35.5 us (9%)
  matrix products  22.6 us (6%)
  blocking collectives  21.3 us (6%)
  other arithmetic  19.1 us (5%)
  between operations  15.4 us (4%)
  local copies, waits for them, and re-layouts  13.2 us (4%)
    all_gather x1, waiting for transfers between devices, sent_together(): lax.all_gather(both, axis, axis=dim, tiled=True)  78.4 us
    all_gather x1, waiting for transfers between devices, local(): lax.all_gather(w_out, SEQ, axis=1, tiled=True)  76.4 us
    all_gather x2, waiting for transfers between devices, prefix_by_axis(): lax.all_gather(part.astype(kind), axis)  36.2 us
    all_to_all x3, waiting for transfers between devices, sent_to_all(): lax.all_to_all(jnp.broadcast_to(shard[None], (count, *shard.shape)), axis...  29.3 us
    all_to_all x1, waiting for transfers between devices, sent_and_summed(): lax.all_to_all(parts, axis, split_axis=0, concat_axis=0, tiled=True)  25.6 us
    all_to_all x3, starting transfers between devices, sent_to_all(): lax.all_to_all(jnp.broadcast_to(shard[None], (count, *shard.shape)), axis...  22.5 us
    unnamed x1, blocking collectives  13.2 us
    dot_general x3, matrix products, local(): jnp.dot(quant, weight_piece, preferred_element_type=jnp.float32)  10.7 us
  transfers between devices with their start and end apart: 10, of which 7 were waited for; matrix products, arithmetic and copies ran while one was open for 10% of the time, Pallas kernels for 0%

commit v1 on v0

--- a/solution.py
+++ b/solution.py
@@ -207,7 +207,9 @@
     mean_sq = squares / (HEADS * HEAD_DIM)
     normed = (ssm_out * lax.rsqrt(mean_sq + epsilon)[:, None] * norm_gain).astype(jnp.bfloat16)
     partial_out = jnp.dot(
-        normed, lax.all_gather(w_out, SEQ, axis=1, tiled=True), preferred_element_type=jnp.float32
+        normed,
+        jnp.concatenate(lax.all_to_all(jnp.stack([w_out] * lax.axis_size(SEQ)), SEQ, 0, 0), axis=1),
+        preferred_element_type=jnp.float32,
     )
     layer_out = sent_and_summed(partial_out.astype(jnp.bfloat16), "tensor", 0).astype(jnp.bfloat16)
     return (layer_out, abs_max)

time: 375 us -> 501 us (1.34)
  waiting for transfers between devices: 247 us -> 362 us
  starting transfers between devices: 35.5 us -> 42.8 us
    all_to_all x0 -> x1, waiting for transfers between devices: none -> 187 us  [local(): lax.all_to_all(jnp.stack([w_out] * lax.axis_size(SEQ)), SEQ, 0, 0)]
    all_gather x1 -> x0, waiting for transfers between devices: 76.4 us -> none  [local(): lax.all_gather(w_out, SEQ, axis=1, tiled=True)]
    all_to_all x0 -> x1, starting transfers between devices: none -> 8.9 us  [local(): lax.all_to_all(jnp.stack([w_out] * lax.axis_size(SEQ)), SEQ, 0, 0)]
  transfers between devices with their start and end apart: 10 -> 10, of which waited for: 7 -> 9; matrix products, arithmetic and copies ran while one was open for 10% -> 5% of each run, Pallas kernels for 0% -> 0%
where the time goes in v1:
time: 501 us; the launch traced here: 500 us
  waiting for transfers between devices  362 us (72%)
  starting transfers between devices  42.8 us (9%)
  matrix products  22.5 us (4%)
  blocking collectives  22.1 us (4%)
  other arithmetic  19.4 us (4%)
  local copies, waits for them, and re-layouts  15.9 us (3%)
  between operations  15.5 us (3%)
    all_to_all x1, waiting for transfers between devices, local(): lax.all_to_all(jnp.stack([w_out] * lax.axis_size(SEQ)), SEQ, 0, 0)  187 us
    all_gather x1, waiting for transfers between devices, sent_together(): lax.all_gather(both, axis, axis=dim, tiled=True)  78.4 us
    all_gather x2, waiting for transfers between devices, prefix_by_axis(): lax.all_gather(part.astype(kind), axis)  38.9 us
    all_to_all x3, waiting for transfers between devices, sent_to_all(): lax.all_to_all(jnp.broadcast_to(shard[None], (count, *shard.shape)), axis...  31.4 us
    all_to_all x1, waiting for transfers between devices, sent_and_summed(): lax.all_to_all(parts, axis, split_axis=0, concat_axis=0, tiled=True)  25.6 us
    all_to_all x3, starting transfers between devices, sent_to_all(): lax.all_to_all(jnp.broadcast_to(shard[None], (count, *shard.shape)), axis...  23.4 us
    unnamed x1, blocking collectives  14 us
    dot_general x3, matrix products, local(): jnp.dot(quant, weight_piece, preferred_element_type=jnp.float32)  10.7 us
  transfers between devices with their start and end apart: 10, of which 9 were waited for; matrix products, arithmetic and copies ran while one was open for 5% of the time, Pallas kernels for 0%

profile of v1, /device:TPU:1, one launch (start us, length us, event | category | flops | bytes accessed | tf_op | source)
XLA Modules:
  0.0 500.1 jit_solution(11263866153296743387)
XLA Ops:
  7.2 0.9 copy.106
  8.1 0.8 copy.72
  8.9 1.7 pad_maximum_fusion.1
  10.6 2.6 broadcast_in_dim.26
  13.2 6.8 %all-to-all-start = ((bf16[8,32,4096]{2,1,0:T(8,128)(2,1)}), bf16[8,32,4096]{2,1,0:T(8,128)(2,1)S(1)}, u32[]{:S(2)}, u32[]{:S(2)}) async-start(bf16[8,32,4096]{2,1,0:T(8,128)(2,1)} %broadcast_in_dim.26), calls=%async_computation | async-start | bytes 4194304 | tf_op jit(solution)/shard_map/all_to_all | solution.py:27
  20.8 25.5 %all-to-all-done = bf16[8,32,4096]{2,1,0:T(8,128)(2,1)S(1)} async-done(((bf16[8,32,4096]{2,1,0:T(8,128)(2,1)}), bf16[8,32,4096]{2,1,0:T(8,128)(2,1)S(1)}, u32[]{:S(2)}, u32[]{:S(2)}) %all-to-all-start) | async-done | bytes 2097184 | tf_op jit(solution)/shard_map/all_to_all | solution.py:27
  46.3 2.6 fusion.5
  48.9 78.4 %all-gather.7.cloned.1.call-done = bf16[4096,1296]{1,0:T(8,128)(2,1)} async-done(((bf16[128,1296]{1,0:T(8,128)(2,1)}), bf16[4096,1296]{1,0:T(8,128)(2,1)}) %all-gather.7.cloned.1.call-update) | async-done | bytes 10616848 | tf_op jit(solution)/shard_map/all_gather | solution.py:47
  127.3 2.7 compare_select_fusion
  130.5 5.7 %fusion.14 = bf16[256,1024]{1,0:T(8,128)(2,1)S(1)} fusion(bf16[256,4096]{1,0:T(8,128)(2,1)S(1)} %bitcast.201, bf16[4096,1296]{1,0:T(8,128)(2,1)} %all-gather.7.cloned.1.call-done, f32[]{:T(128)S(6)} %div.21), kind=kOutput, calls=%fused_computation.23 | convolution fusion | flops 2148007936 | bytes 11010052 | tf_op jit(solution)/shard_map/dot_general | solution.py:140
  136.2 1.6 collective-permute-start
  137.8 2.3 fusion.20
  140.1 3.2 collective-permute-start.1
  143.3 0.6 subtract_exponential_fusion
  144.3 0.8 fusion.93
  145.1 2.6 multiply_convert_fusion.3
  147.8 0.7 reshape.429
  148.4 0.9 copy.80
  149.7 2.0 while.13
  149.7 0.8 bitcast_dynamic-update-slice_fusion.2
  150.7 0.8 bitcast_dynamic-update-slice_fusion.2
  151.7 0.8 add_convert_fusion
  152.7 0.6 dynamic-slice
  154.1 14.0 %all-reduce = bf16[128]{0:T(256)(128)(2,1)S(1)} all-reduce(bf16[128]{0:T(256)(128)(2,1)S(1)} %dynamic-update-slice), channel_id=2, replica_groups=mesh['seq_0'=4,'seq_1'=8,'tensor'=8] {'seq_1'}, use_global_device_ids=true, to_apply=%add | all-reduce | flops 128 | bytes 512
  168.2 0.6 broadcast_select_fusion.8
  168.9 22.7 %all-gather.11.cloned.1.call-done = bf16[128,64,128]{2,1,0:T(8,128)(2,1)} async-done(((bf16[16,64,128]{2,1,0:T(8,128)(2,1)}), bf16[128,64,128]{2,1,0:T(8,128)(2,1)}) %all-gather.11.cloned.1.call-update) | async-done | bytes 2097168 | tf_op jit(solution)/shard_map/all_gather | solution.py:68
  191.6 2.8 fusion.77
  194.5 8.1 %all-gather.2 = bf16[4,1,16]{2,1,0:T(2,128)(2,1)S(1)} all-gather(bf16[1,1,16]{2,1,0:T(2,128)(2,1)S(1)} %fusion.88), channel_id=1, replica_groups=mesh['seq_0'=4,'seq_1'=8,'tensor'=8] {'seq_0'}, dimensions={0}, use_global_device_ids=true | all-gather | bytes 160 | tf_op jit(solution)/shard_map/all_gather | solution.py:68
  202.7 1.1 copy.108
  204.0 1.9 convolution_bitcast_fusion.1
  205.9 16.1 %all-gather.9.cloned.1.call-done = bf16[4,16,64,128]{3,2,1,0:T(8,128)(2,1)} async-done(((bf16[1,16,64,128]{3,2,1,0:T(8,128)(2,1)}), bf16[4,16,64,128]{3,2,1,0:T(8,128)(2,1)}) %all-gather.9.cloned.1.call-update) | async-done | bytes 1048592 | tf_op jit(solution)/shard_map/all_gather | solution.py:68
  222.1 3.1 fusion.44
  225.2 2.2 multiply_reduce_fusion
  227.4 0.6 broadcast_in_dim.33
  228.0 7.0 %all-to-all-start.1 = ((f32[8,1,256]{2,1,0:T(1,128)}), f32[8,1,256]{2,1,0:T(1,128)S(1)}, u32[]{:S(2)}, u32[]{:S(2)}) async-start(f32[8,1,256]{2,1,0:T(1,128)} %broadcast_in_dim.33), calls=%async_computation.1 | async-start | bytes 16384 | tf_op jit(solution)/shard_map/all_to_all | solution.py:27
  235.2 4.5 all-to-all-done.1
  239.7 4.3 stack.2
  244.0 8.9 %all-to-all-start.2 = ((bf16[32,1024,128]{1,2,0:T(8,128)(2,1)}), bf16[32,1024,128]{1,2,0:T(8,128)(2,1)}, u32[]{:S(2)}, u32[]{:S(2)}) async-start(bf16[32,1024,128]{1,2,0:T(8,128)(2,1)} %stack.2), calls=%async_computation.2 | async-start | bytes 16777216 | tf_op jit(solution)/shard_map/all_to_all | solution.py:211
  253.3 0.5 copy.86
  253.8 187.4 %all-to-all-done.2 = bf16[32,1024,128]{1,2,0:T(8,128)(2,1)} async-done(((bf16[32,1024,128]{1,2,0:T(8,128)(2,1)}), bf16[32,1024,128]{1,2,0:T(8,128)(2,1)}, u32[]{:S(2)}, u32[]{:S(2)}) %all-to-all-start.2) | async-done | bytes 8388640 | tf_op jit(solution)/shard_map/all_to_all | solution.py:211
  441.2 1.3 broadcast_in_dim.35
  442.4 9.6 %all-to-all-start.4 = ((f32[32,1,1]{2,1,0:T(1,128)}), f32[32,1,1]{2,1,0:T(1,128)S(1)}, u32[]{:S(2)}, u32[]{:S(2)}) async-start(f32[32,1,1]{2,1,0:T(1,128)} %broadcast_in_dim.35), calls=%async_computation.4 | async-start | bytes 32768 | tf_op jit(solution)/shard_map/all_to_all | solution.py:27
  452.0 7.2 %convolution_convert_fusion = bf16[256,4096]{1,0:T(8,128)(2,1)} fusion(bf16[1024,4096]{0,1:T(8,128)(2,1)} %bitcast.39, bf16[128,8,2,128]{3,2,1,0:T(2,128)(2,1)S(1)} %bitcast.209), kind=kOutput, calls=%fused_computation.8 | convolution fusion | flops 2148532224 | bytes 11010048 | tf_op jit(solution)/shard_map/dot_general | solution.py:209
  459.1 1.4 all-to-all-done.4
  460.6 5.7 %all-to-all-start.3 = ((bf16[8,32,4096]{2,1,0:T(8,128)(2,1)}), bf16[8,32,4096]{2,1,0:T(8,128)(2,1)S(1)}, u32[]{:S(2)}, u32[]{:S(2)}) async-start(bf16[8,32,4096]{2,1,0:T(8,128)(2,1)} %bitcast.203), calls=%async_computation.3 | async-start | bytes 4194304 | tf_op jit(solution)/shard_map/all_to_all | solution.py:94
  466.2 0.6 reduce_max.19
  466.9 25.6 %all-to-all-done.3 = bf16[8,32,4096]{2,1,0:T(8,128)(2,1)S(1)} async-done(((bf16[8,32,4096]{2,1,0:T(8,128)(2,1)}), bf16[8,32,4096]{2,1,0:T(8,128)(2,1)S(1)}, u32[]{:S(2)}, u32[]{:S(2)}) %all-to-all-start.3) | async-done | bytes 2097184 | tf_op jit(solution)/shard_map/all_to_all | solution.py:94
  492.5 1.1 reduce_sum.42
  (89 shorter events, 3.0 us)
Async XLA Ops:
  7.2 120.2 %all-gather.7.cloned.1.call-start = ((), (), s32[]{:S(2)}) async-start(), calls=%async_computation.5 | async-start | bytes 11894784 | tf_op jit(solution)/shard_map/all_gather | solution.py:47
  13.2 7.5 %copy-start.12 = (f32[4,1,2,128]{3,2,1,0:T(2,128)S(1)}, f32[4,1,2,128]{3,2,1,0:T(2,128)}, u32[]{:S(2)}) copy-start(f32[4,1,2,128]{3,2,1,0:T(2,128)} %param.23) | copy-start | bytes 12292
  13.2 7.6 %copy-start.7 = (f32[4,1024]{1,0:T(4,128)S(1)}, f32[4,1024]{1,0:T(4,128)}, u32[]{:S(2)}) copy-start(f32[4,1024]{1,0:T(4,128)} %param.22) | copy-start | bytes 49156
  13.2 33.1 %all-to-all-start = ((bf16[8,32,4096]{2,1,0:T(8,128)(2,1)}), bf16[8,32,4096]{2,1,0:T(8,128)(2,1)S(1)}, u32[]{:S(2)}, u32[]{:S(2)}) async-start(bf16[8,32,4096]{2,1,0:T(8,128)(2,1)} %broadcast_in_dim.26), calls=%async_computation | async-start | bytes 4194304 | tf_op jit(solution)/shard_map/all_to_all | solution.py:27
  20.1 171.5 %all-gather.11.cloned.1.call-start = ((), (), s32[]{:S(2)}) async-start(), calls=%async_computation.7 | async-start | bytes 2359296 | tf_op jit(solution)/shard_map/all_gather | solution.py:68
  20.8 106.5 %copy-start.16 = (f32[16]{0:T(128)S(1)}, f32[16]{0:T(128)}, u32[]{:S(2)}) copy-start(f32[16]{0:T(128)} %param.26) | copy-start | bytes 196
  48.9 81.2 %copy-start.17 = (f32[16]{0:T(128)S(1)}, f32[16]{0:T(128)}, u32[]{:S(2)}) copy-start(f32[16]{0:T(128)} %param.27) | copy-start | bytes 196
  127.3 3.1 copy-start
  136.2 3.9 copy-start.5
  136.2 7.8 %copy-start.15 = (bf16[3,1,2,128]{3,2,1,0:T(2,128)(2,1)S(1)}, bf16[3,1,2,128]{3,2,1,0:T(2,128)(2,1)}, u32[]{:S(2)}) copy-start(bf16[3,1,2,128]{3,2,1,0:T(2,128)(2,1)} %param.25) | copy-start | bytes 4612
  136.2 8.9 %copy-start.8 = (bf16[3,1024]{1,0:T(4,128)(2,1)S(1)}, bf16[3,1024]{1,0:T(4,128)(2,1)}, u32[]{:S(2)}) copy-start(bf16[3,1024]{1,0:T(4,128)(2,1)} %param.24) | copy-start | bytes 18436
  136.2 8.9 %collective-permute-start = (bf16[3,1024]{1,0:T(4,128)(2,1)S(1)}, bf16[3,1024]{1,0:T(4,128)(2,1)S(1)}, u32[]{:S(2)}, u32[]{:S(2)}) collective-permute-start(bf16[3,1024]{1,0:T(4,128)(2,1)S(1)} %slice.196), channel_id=1, source_target_pairs={{0,8},{8,16},{16,24},{24,32},{32,40},{40,48},{48,56},{56,64},{64,7... | collective-permute-start | bytes 18440 | tf_op jit(solution)/shard_map/ppermute | solution.py:53
  140.1 3.9 collective-permute-start.1
  149.7 2.0 copy-start.2
  149.7 3.0 copy-start.19
  152.6 69.5 %all-gather.9.cloned.1.call-start = ((), (), s32[]{:S(2)}) async-start(), calls=%async_computation.6 | async-start | bytes 1310720 | tf_op jit(solution)/shard_map/all_gather | solution.py:68
  168.8 33.8 %copy-start.9 = (f32[16]{0:T(128)}, f32[16]{0:T(128)S(1)}, u32[]{:S(2)}) copy-start(f32[16]{0:T(128)S(1)} %get-tuple-element.82) | copy-start | bytes 196
  202.7 19.3 %copy-start.1 = (bf16[128,64,128]{2,1,0:T(8,128)(2,1)S(1)}, bf16[128,64,128]{2,1,0:T(8,128)(2,1)}, u32[]{:S(2)}) copy-start(bf16[128,64,128]{2,1,0:T(8,128)(2,1)} %all-gather.11.cloned.1.call-done) | copy-start | bytes 6291460
  202.7 19.3 %copy-start.10 = (f32[16]{0:T(128)S(1)}, f32[16]{0:T(128)}, u32[]{:S(2)}) copy-start(f32[16]{0:T(128)} %copy-done.9) | copy-start | bytes 196
  202.7 19.3 %copy-start.14 = (f32[16]{0:T(128)S(1)}, f32[16]{0:T(128)}, u32[]{:S(2)}) copy-start(f32[16]{0:T(128)} %get-tuple-element.81) | copy-start | bytes 196
  222.0 3.2 copy-start.3
  222.0 3.2 copy-start.4
  222.0 3.2 copy-start.13
  222.1 3.2 copy-start.18
  225.2 9.9 %copy-start.6 = (bf16[1024,128]{1,0:T(8,128)(2,1)S(1)}, bf16[1024,128]{1,0:T(8,128)(2,1)}, u32[]{:S(2)}) copy-start(bf16[1024,128]{1,0:T(8,128)(2,1)} %param.31) | copy-start | bytes 786436
  228.0 11.7 %all-to-all-start.1 = ((f32[8,1,256]{2,1,0:T(1,128)}), f32[8,1,256]{2,1,0:T(1,128)S(1)}, u32[]{:S(2)}, u32[]{:S(2)}) async-start(f32[8,1,256]{2,1,0:T(1,128)} %broadcast_in_dim.33), calls=%async_computation.1 | async-start | bytes 16384 | tf_op jit(solution)/shard_map/all_to_all | solution.py:27
  244.0 8.9 %copy-start.11 = (f32[1024]{0:T(1024)S(1)}, f32[1024]{0:T(1024)}, u32[]{:S(2)}) copy-start(f32[1024]{0:T(1024)} %param.30) | copy-start | bytes 12292
  244.0 197.2 %all-to-all-start.2 = ((bf16[32,1024,128]{1,2,0:T(8,128)(2,1)}), bf16[32,1024,128]{1,2,0:T(8,128)(2,1)}, u32[]{:S(2)}, u32[]{:S(2)}) async-start(bf16[32,1024,128]{1,2,0:T(8,128)(2,1)} %stack.2), calls=%async_computation.2 | async-start | bytes 16777216 | tf_op jit(solution)/shard_map/all_to_all | solution.py:211
  442.4 18.2 %all-to-all-start.4 = ((f32[32,1,1]{2,1,0:T(1,128)}), f32[32,1,1]{2,1,0:T(1,128)S(1)}, u32[]{:S(2)}, u32[]{:S(2)}) async-start(f32[32,1,1]{2,1,0:T(1,128)} %broadcast_in_dim.35), calls=%async_computation.4 | async-start | bytes 32768 | tf_op jit(solution)/shard_map/all_to_all | solution.py:27
  460.6 31.9 %all-to-all-start.3 = ((bf16[8,32,4096]{2,1,0:T(8,128)(2,1)}), bf16[8,32,4096]{2,1,0:T(8,128)(2,1)S(1)}, u32[]{:S(2)}, u32[]{:S(2)}) async-start(bf16[8,32,4096]{2,1,0:T(8,128)(2,1)} %bitcast.203), calls=%async_computation.3 | async-start | bytes 4194304 | tf_op jit(solution)/shard_map/all_to_all | solution.py:94
Sparse Core Ops, SparseCore 0:
  10.7 116.5 all-gather.6
  152.7 38.8 all-gather.10
  194.5 27.4 all-gather.8
